TPU v7x, 256 devices: a whole 4x4x8 slice. The times are simulated.
256 devices in a mesh: dp: 4 (over x), expert: 64 (over z, y, core).
Axes of the slice: x: 4, y: 4, z: 8, core: 2. Of those that a mesh axis runs over, the one named last changes fastest.
Arguments:
- queries: bfloat16 [16384, 2048], P('expert', 'dp'), may hold values from -160 to 160
- kv_pool: bfloat16 [2, 1024, 64, 2048], P(None, 'expert', None, 'dp'), may hold values from -6 to 6
- page_table: int32 [256, 4], P('expert'), may hold values from 0 to 1023, as said below
- ctx_lens: int32 [16384], P('expert'), may hold values from 2 to 256, as said below
- w_out: bfloat16 [2048, 2048], P('dp', 'expert'), may hold values from -0.59765625 to 0.59765625
- residual: bfloat16 [16384, 2048], P(('expert', 'dp')), may hold values from -3 to 3
- moe_gain: float32 [2048], replicated, may hold values from 0.25 to 1.75
- expert_ids: int32 [16384, 6], P(('expert', 'dp')), may hold values from 0 to 63, all different within a row; in each aligned block of 64 rows (0 to 63, 64 to 127, ...) at most 12 rows name the same one
- route_weights: float32 [16384, 6], P(('expert', 'dp')), may hold values from 0.05 to 0.4
- w_gate: bfloat16 [64, 2048, 1408], P('expert', 'dp'), may hold values from -0.125 to 0.125
- w_up: bfloat16 [64, 2048, 1408], P('expert', 'dp'), may hold values from -0.125 to 0.125
- w_down: bfloat16 [64, 1408, 2048], P('expert', 'dp'), may hold values from -0.15625 to 0.15625
- final_gain: float32 [2048], replicated, may hold values from 0.25 to 1.75
Outputs:
- layer_out: bfloat16 [16384, 2048], P(('expert', 'dp'))
Inputs may be any that keep to these rules, and one draw needn't show every extreme that they name: `page_table`: the 4 pages of sequence s are distinct pages of group s // 4, which owns pages g * 16 to g * 16 + 15; every page belongs to exactly one sequence. `ctx_lens`: the first row of every sequence reads all 256 positions. `expert_ids`: each row names 6 distinct experts; among the 64 rows of one device (aligned blocks of 64 rows) no expert is named more than 12 times.
All inputs are finite; a program needn't handle non-finite values.
Results may differ from a plain program's by a relative error of at most 0.017.
Values may be sent and summed in bfloat16 or wider, within the bound.
A program may use at most 128 MiB of HBM per device.

v0:
```python
import math
import jax
import jax.numpy as jnp
from jax import lax
from jax.sharding import PartitionSpec as P

HD = 128
TOP = 6
CTX = 256


def normalize(values, gain):
    mean_sq = jnp.mean(values * values, axis=-1, keepdims=True)
    return values * lax.rsqrt(mean_sq + 1e-06) * gain


def fetch_experts(w_gate, w_up, w_down):
    return (
        lax.all_gather(w_gate, "dp", axis=1, tiled=True),
        lax.all_gather(w_up, "dp", axis=1, tiled=True),
        lax.all_gather(w_down, "dp", axis=1, tiled=True),
    )


def shards(
    queries,
    kv_pool,
    page_table,
    ctx_lens,
    w_out,
    residual,
    moe_gain,
    expert_ids,
    route_weights,
    w_gate,
    w_up,
    w_down,
    final_gain,
):
    replicas = None
    scale = 1.0 / math.sqrt(HD)
    group_rows = queries.shape[0]
    local_feats = queries.shape[1]
    local_heads = local_feats // HD
    seq_count = page_table.shape[0]
    seq_rows = group_rows // seq_count
    pool_here = kv_pool.shape[1]
    local_pages = page_table - lax.axis_index("expert") * pool_here
    keys = kv_pool[0][local_pages].reshape(seq_count, CTX, local_heads, HD)
    values = kv_pool[1][local_pages].reshape(seq_count, CTX, local_heads, HD)
    asked = queries.reshape(seq_count, seq_rows, local_heads, HD)
    scores = jnp.einsum("sqhd,skhd->shqk", asked, keys, preferred_element_type=jnp.float32) * scale
    lengths = ctx_lens.reshape(seq_count, seq_rows)
    visible = (jnp.arange(CTX, dtype=jnp.int32)[None, None, :] < lengths[:, :, None])[:, None]
    scores = jnp.where(visible, scores, -1e30)
    top_score = jnp.max(scores, axis=-1, keepdims=True)
    expo = jnp.where(visible, jnp.exp(scores - top_score), 0.0)
    probs = (expo / jnp.sum(expo, axis=-1, keepdims=True)).astype(jnp.bfloat16)
    mixed = jnp.einsum("shqk,skhd->sqhd", probs, values, preferred_element_type=jnp.float32)
    context = mixed.astype(jnp.bfloat16).reshape(group_rows, local_feats)
    columns = lax.all_gather(w_out, "expert", axis=1, tiled=True)
    projected = lax.psum_scatter(
        jnp.dot(context, columns, preferred_element_type=jnp.float32).astype(jnp.bfloat16),
        "dp",
        scatter_dimension=0,
        tiled=True,
    ).astype(jnp.float32)
    hidden_state = residual.astype(jnp.float32) + projected
    moe_input = normalize(hidden_state, moe_gain).astype(jnp.bfloat16)
    rows_here = moe_input.shape[0]
    experts = lax.axis_size("expert")
    slots = max(2, min(rows_here, 2 * rows_here * TOP // experts))
    flat_ids = expert_ids.reshape(-1)
    marks = (flat_ids[:, None] == jnp.arange(experts, dtype=jnp.int32)[None, :]).astype(jnp.int32)
    before = jnp.sum((jnp.cumsum(marks, axis=0) - 1) * marks, axis=1)
    target = (flat_ids * slots + before).reshape(rows_here, TOP)
    placing = jnp.any(
        jnp.arange(experts * slots, dtype=jnp.int32)[:, None, None] == target[None], axis=-1
    )
    outbound = jnp.dot(placing.astype(jnp.bfloat16), moe_input, preferred_element_type=jnp.float32)
    outbound = outbound.astype(jnp.bfloat16).reshape(experts, slots, moe_input.shape[1])
    replicas = fetch_experts(w_gate, w_up, w_down)
    gate_full, up_full, down_full = replicas
    arrived = lax.all_to_all(outbound, "expert", split_axis=0, concat_axis=0, tiled=True)
    flat = arrived.reshape(-1, arrived.shape[2])
    gate = jnp.dot(flat, gate_full[0], preferred_element_type=jnp.float32)
    up_part = jnp.dot(flat, up_full[0], preferred_element_type=jnp.float32)
    expert_mid = (jax.nn.silu(gate) * up_part).astype(jnp.bfloat16)
    done = jnp.dot(expert_mid, down_full[0], preferred_element_type=jnp.float32).astype(
        jnp.bfloat16
    )
    done = done.reshape(arrived.shape[0], arrived.shape[1], arrived.shape[2])
    returned = lax.all_to_all(done, "expert", split_axis=0, concat_axis=0, tiled=True)
    answers = returned.reshape(experts * slots, returned.shape[2])[target]
    moe = jnp.sum(route_weights[:, :, None] * answers.astype(jnp.float32), axis=1)
    combined = hidden_state + moe
    return normalize(combined, final_gain).astype(jnp.bfloat16)


def solution(mesh):
    return jax.shard_map(
        shards,
        mesh=mesh,
        in_specs=(
            P("expert", "dp"),
            P(None, "expert", None, "dp"),
            P("expert", None),
            P("expert"),
            P("dp", "expert"),
            P(("expert", "dp"), None),
            P(),
            P(("expert", "dp"), None),
            P(("expert", "dp"), None),
            P("expert", "dp", None),
            P("expert", "dp", None),
            P("expert", "dp", None),
            P(),
        ),
        out_specs=P(("expert", "dp"), None),
        check_vma=False,
    )
```

profile of v0, /device:TPU:8, one launch (start us, length us, event | category | flops | bytes accessed | tf_op | source)
XLA Modules:
  0.0 469.7 jit_solution(8235177650475701003)
XLA Ops:
  6.5 0.0 all-gather.5.cloned.1.call-start
  6.5 0.7 all-gather.5.cloned.1.call-update
  7.3 0.0 reduce-scatter.2.cloned.1.call-start
  7.3 0.7 compare_select_fusion.1
  8.0 0.1 reshape.88
  8.1 0.0 copy-start.8
  8.1 1.7 slice_bitcast_fusion
  9.9 0.6 gather_fusion.1
  10.5 0.3 reshape.78
  10.8 0.0 copy-done.2
  10.8 0.8 reshape.79
  11.5 0.0 copy-done.8
  11.6 0.1 lt.31
  11.6 0.6 gather_fusion
  12.3 0.3 reshape.77
  12.6 0.1 iota_compare_fusion.1
  12.7 0.0 copy-done.3
  12.7 1.6 fusion.34
  14.3 1.6 fusion.18
  15.9 0.2 copy.43
  16.1 73.2 %all-gather.5.cloned.1.call-done = bf16[512,2048]{0,1:T(8,128)(2,1)} async-done(((bf16[512,32]{0,1:T(8,128)(2,1)}), bf16[512,2048]{0,1:T(8,128)(2,1)}) %all-gather.5.cloned.1.call-update) | async-done | bytes 2097168 | tf_op jit(solution)/shard_map/all_gather | solution.py:61
  89.3 3.4 convolution_convert_fusion.1
  92.7 0.0 reduce-scatter.2.cloned.1.call-update
  92.7 0.0 all-gather.9.cloned.1.call-start
  92.8 0.7 all-gather.9.cloned.1.call-update
  93.5 0.0 all-gather.11.cloned.1.call-start
  93.5 0.5 all-gather.11.cloned.1.call-update
  94.0 0.0 all-gather.7.cloned.1.call-start
  94.1 0.5 all-gather.7.cloned.1.call-update
  94.6 0.0 copy-done.4
  94.6 0.1 copy.45
  94.7 0.1 eq.43
  94.9 0.1 eq.39
  95.0 0.9 reduce-window.6
  95.9 0.2 slice_reduce_fusion
  96.2 0.1 fusion.31
  96.3 0.1 reduce_sum.49
  96.5 0.1 copy.48
  96.5 0.3 fusion.17
  96.8 20.8 %reduce-scatter.2.cloned.1.call-done = bf16[64,2048]{1,0:T(8,128)(2,1)} async-done(((bf16[256,2048]{1,0:T(8,128)(2,1)}), bf16[64,2048]{1,0:T(8,128)(2,1)}) %reduce-scatter.2.cloned.1.call-update) | async-done | bytes 262160 | tf_op jit(solution)/shard_map/reduce_scatter | solution.py:62
  117.6 0.0 copy-done
  117.6 1.1 multiply_reduce_fusion.2
  118.7 0.0 copy-done.5
  118.8 2.0 convolution_convert_fusion
  120.8 2.7 reshape.82
  123.4 106.9 %all_to_all.10 = bf16[64,12,2048]{2,1,0:T(8,128)(2,1)} all-to-all(bf16[64,12,2048]{2,1,0:T(8,128)(2,1)} %reshape.82), channel_id=1, replica_groups=mesh['dp'=4,'expert'=64] {'expert'}, dimensions={0} | all-to-all | bytes 6291456 | tf_op jit(solution)/shard_map/all_to_all | solution.py:84
  230.3 4.7 %reshape.83 = bf16[768,2048]{1,0:T(8,128)(2,1)S(1)} reshape(bf16[64,12,2048]{2,1,0:T(8,128)(2,1)} %all_to_all.10) | data formatting | bytes 6291456 | tf_op jit(solution)/shard_map/reshape | solution.py:85
  235.1 0.0 all-gather.9.cloned.1.call-done
  235.1 9.3 %fusion.3 = f32[768,1408]{1,0:T(8,128)} fusion(bf16[768,2048]{1,0:T(8,128)(2,1)S(1)} %reshape.83, bf16[1,2048,1408]{2,1,0:T(8,128)(2,1)} %all-gather.9.cloned.1.call-done), kind=kOutput, calls=%fused_computation.6 | convolution fusion | flops 4429185024 | bytes 13238272 | tf_op jit(solution)/shard_map/dot_general | solution.py:87
  244.4 5.2 %all-gather.11.cloned.1.call-done = bf16[1,1408,2048]{2,1,0:T(8,128)(2,1)} async-done(((bf16[1,352,2048]{2,1,0:T(8,128)(2,1)}), bf16[1,1408,2048]{2,1,0:T(8,128)(2,1)}) %all-gather.11.cloned.1.call-update) | async-done | bytes 5767184 | tf_op jit(solution)/shard_map/all_gather | solution.py:21
  249.6 66.3 %all-gather.7.cloned.1.call-done = bf16[1,2048,1408]{2,1,0:T(8,128)(2,1)} async-done(((bf16[1,512,1408]{2,1,0:T(8,128)(2,1)}), bf16[1,2048,1408]{2,1,0:T(8,128)(2,1)}) %all-gather.7.cloned.1.call-update) | async-done | bytes 5767184 | tf_op jit(solution)/shard_map/all_gather | solution.py:19
  315.9 17.6 %fusion.9 = bf16[768,2048]{1,0:T(8,128)(2,1)} fusion(bf16[1,1408,2048]{2,1,0:T(8,128)(2,1)} %all-gather.11.cloned.1.call-done, f32[768,1408]{1,0:T(8,128)} %fusion.3, bf16[768,2048]{1,0:T(8,128)(2,1)S(1)} %reshape.83, bf16[1,2048,1408]{2,1,0:T(8,128)(2,1)} %all-gather.7.cloned.1.call-done), kind=kOutput, calls=%fused_computation.13 | convolution fusion | flops 8866430976 | bytes 22151168 | tf_op jit(solution)/shard_map/dot_general | solution.py:89
  333.5 6.1 %reshape.84 = bf16[64,12,2048]{2,1,0:T(8,128)(2,1)} reshape(bf16[768,2048]{1,0:T(8,128)(2,1)} %fusion.9) | data formatting | bytes 6291456 | tf_op jit(solution)/shard_map/reshape | solution.py:92
  339.5 10.9 %all-to-all-start.1 = ((bf16[64,12,2048]{2,1,0:T(8,128)(2,1)}), bf16[64,12,2048]{2,1,0:T(8,128)(2,1)}, u32[]{:S(2)}, u32[]{:S(2)}) async-start(bf16[64,12,2048]{2,1,0:T(8,128)(2,1)} %reshape.84), calls=%async_computation.2 | async-start | bytes 8388608 | tf_op jit(solution)/shard_map/all_to_all | solution.py:93
  350.4 0.1 copy.49
  350.5 0.1 reshape.104
  350.7 0.1 copy.44
  350.8 95.8 %all-to-all-done.1 = bf16[64,12,2048]{2,1,0:T(8,128)(2,1)} async-done(((bf16[64,12,2048]{2,1,0:T(8,128)(2,1)}), bf16[64,12,2048]{2,1,0:T(8,128)(2,1)}, u32[]{:S(2)}, u32[]{:S(2)}) %all-to-all-start.1) | async-done | bytes 3145760 | tf_op jit(solution)/shard_map/all_to_all | solution.py:93
  446.5 4.7 %reshape.85 = bf16[768,2048]{1,0:T(8,128)(2,1)S(1)} reshape(bf16[64,12,2048]{2,1,0:T(8,128)(2,1)} %all-to-all-done.1) | data formatting | bytes 6291456 | tf_op jit(solution)/shard_map/reshape | solution.py:94
  451.3 3.1 gather_fusion.2
  454.4 3.9 reshape.118
  458.3 3.7 multiply_reduce_fusion
  462.1 0.2 multiply_reduce_fusion.1
  462.3 0.8 multiply_convert_fusion.1
  (18 shorter events, 0.1 us)
Async XLA Ops:
  6.5 82.8 %all-gather.5.cloned.1.call-start = ((), (), s32[]{:S(2)}) async-start(), calls=%async_computation.3 | async-start | bytes 2129920 | tf_op jit(solution)/shard_map/all_gather | solution.py:61
  7.3 110.3 %reduce-scatter.2.cloned.1.call-start = ((), (), s32[]{:S(2)}) async-start(), calls=%async_computation.4 | async-start | bytes 1310720 | tf_op jit(solution)/shard_map/reduce_scatter | solution.py:62
  8.1 2.7 copy-start.2
  8.1 3.5 copy-start.8
  11.6 1.1 copy-start.3
  89.3 5.3 %copy-start.4 = (s32[64,6]{0,1:T(8,128)S(1)}, s32[64,6]{0,1:T(8,128)}, u32[]{:S(2)}) copy-start(s32[64,6]{0,1:T(8,128)} %param.20) | copy-start | bytes 4612
  89.3 28.3 %copy-start = (bf16[64,2048]{1,0:T(8,128)(2,1)S(1)}, bf16[64,2048]{1,0:T(8,128)(2,1)}, u32[]{:S(2)}) copy-start(bf16[64,2048]{1,0:T(8,128)(2,1)} %param.18) | copy-start | bytes 786436
  89.3 29.4 %copy-start.5 = (f32[2048]{0:T(1024)S(1)}, f32[2048]{0:T(1024)}, u32[]{:S(2)}) copy-start(f32[2048]{0:T(1024)} %param.19) | copy-start | bytes 24580
  92.7 142.3 %all-gather.9.cloned.1.call-start = ((), (), s32[]{:S(2)}) async-start(), calls=%async_computation.6 | async-start | bytes 7208960 | tf_op jit(solution)/shard_map/all_gather | solution.py:20
  93.5 156.1 %all-gather.11.cloned.1.call-start = ((), (), s32[]{:S(2)}) async-start(), calls=%async_computation.7 | async-start | bytes 7208960 | tf_op jit(solution)/shard_map/all_gather | solution.py:21
  94.0 221.8 %all-gather.7.cloned.1.call-start = ((), (), s32[]{:S(2)}) async-start(), calls=%async_computation.5 | async-start | bytes 7208960 | tf_op jit(solution)/shard_map/all_gather | solution.py:19
  339.5 11.1 %copy-start.7 = (f32[64,6]{0,1:T(8,128)S(1)}, f32[64,6]{0,1:T(8,128)}, u32[]{:S(2)}) copy-start(f32[64,6]{0,1:T(8,128)} %param.21) | copy-start | bytes 4612
  339.5 107.0 %all-to-all-start.1 = ((bf16[64,12,2048]{2,1,0:T(8,128)(2,1)}), bf16[64,12,2048]{2,1,0:T(8,128)(2,1)}, u32[]{:S(2)}, u32[]{:S(2)}) async-start(bf16[64,12,2048]{2,1,0:T(8,128)(2,1)} %reshape.84), calls=%async_computation.2 | async-start | bytes 8388608 | tf_op jit(solution)/shard_map/all_to_all | solution.py:93
  454.4 7.7 %copy-start.1 = (bf16[64,2048]{1,0:T(8,128)(2,1)S(1)}, bf16[64,2048]{1,0:T(8,128)(2,1)}, u32[]{:S(2)}) copy-start(bf16[64,2048]{1,0:T(8,128)(2,1)} %reduce-scatter.2.cloned.1.call-done) | copy-start | bytes 786436
  458.3 4.0 copy-start.6
Sparse Core Ops, SparseCore 0:
  10.1 79.1 all-gather.4
  92.8 24.6 reduce-scatter.1
  119.6 63.6 all-gather.8
  185.1 64.4 all-gather.10
  251.4 64.4 all-gather.6
where the time goes:
time: 471 us; the launch traced here: 470 us
  waiting for transfers between devices  264 us (56%)
  blocking collectives  107 us (23%)
  matrix products  35.4 us (8%)
  local copies, waits for them, and re-layouts  31.1 us (7%)
  between operations  13.4 us (3%)
  starting transfers between devices  11 us (2%)
  other arithmetic  8.07 us (2%)
    all_to_all x1, blocking collectives, shards(): lax.all_to_all(outbound, 'expert', split_axis=0, concat_axis=0, tiled=True)  107 us
    all_to_all x1, waiting for transfers between devices, shards(): lax.all_to_all(done, 'expert', split_axis=0, concat_axis=0, tiled=True)  95.8 us
    all_gather x1, waiting for transfers between devices, shards(): columns = lax.all_gather(w_out, 'expert', axis=1, tiled=True)  73.2 us
    all_gather x1, waiting for transfers between devices, fetch_experts(): lax.all_gather(w_gate, 'dp', axis=1, tiled=True)  66.3 us
    reduce_scatter x1, waiting for transfers between devices, shards(): lax.psum_scatter(jnp.dot(context, columns, preferred_element_type=jnp.flo...  20.8 us
    dot_general x1, matrix products, shards(): jnp.dot(expert_mid, down_full[0], preferred_element_type=jnp.float32)  17.6 us
    all_to_all x1, starting transfers between devices, shards(): lax.all_to_all(done, 'expert', split_axis=0, concat_axis=0, tiled=True)  10.9 us
  transfers between devices with their start and end apart: 6, of which 5 were waited for; matrix products, arithmetic and copies ran while one was open for 7% of the time, Pallas kernels for 0%

commit v1 on v0

--- a/solution.py
+++ b/solution.py
@@ -1,3 +1,4 @@
+import functools
 import math
 import jax
 import jax.numpy as jnp
@@ -9,6 +10,25 @@
 CTX = 256
 
 
+def state_slot_on(in_array, axis_no):
+    degree = lax.psum(1, "dp")
+    all_rows = tuple(((no, (no + 1) % degree) for no in range(degree)))
+    sides = tuple(((no, (no - 1) % degree) for no in range(degree)))
+    piece_out, z_new = ([in_array], [in_array])
+    for _ in range(degree // 2):
+        y2 = lax.ppermute(piece_out[-1], "dp", all_rows)
+        piece_out.append(y2)
+    for _ in range((degree - 1) // 2):
+        z_new.append(lax.ppermute(z_new[-1], "dp", sides))
+    passed = jnp.concatenate([*piece_out[::-1], *z_new[1:]], axis=axis_no)
+    return jnp.roll(
+        passed, (lax.axis_index("dp") - degree // 2) * in_array.shape[axis_no], axis=axis_no
+    )
+
+
+review_row = functools.partial(state_slot_on, axis_no=1)
+
+
 def normalize(values, gain):
     mean_sq = jnp.mean(values * values, axis=-1, keepdims=True)
     return values * lax.rsqrt(mean_sq + 1e-06) * gain
@@ -16,7 +36,7 @@
 
 def fetch_experts(w_gate, w_up, w_down):
     return (
-        lax.all_gather(w_gate, "dp", axis=1, tiled=True),
+        review_row(w_gate),
         lax.all_gather(w_up, "dp", axis=1, tiled=True),
         lax.all_gather(w_down, "dp", axis=1, tiled=True),
     )

time: 471 us -> 446 us (0.947)
  blocking collectives: 107 us -> 0 us
  waiting for transfers between devices: 264 us -> 316 us
  local copies, waits for them, and re-layouts: 31.1 us -> 46.5 us
  starting transfers between devices: 11 us -> 25.2 us
    ppermute x0 -> x3, waiting for transfers between devices: none -> 107 us  [the longest x2 107 us: state_slot_on(): y2 = lax.ppermute(piece_out[-1], 'dp', all_rows)]
    all_to_all x1 -> x0, blocking collectives: 107 us -> none  [shards(): lax.all_to_all(outbound, 'expert', split_axis=0, concat_axis=0, tiled=True)]
    all_gather x1 -> x0, waiting for transfers between devices: 66.3 us -> none  [fetch_experts(): lax.all_gather(w_gate, 'dp', axis=1, tiled=True)]
    unnamed x20 -> x27, local copies, waits for them, and re-layouts: 0.23 us -> 13 us
    all_gather x1, waiting for transfers between devices: 5.21 us -> 17.2 us  [fetch_experts(): lax.all_gather(w_down, 'dp', axis=1, tiled=True)]
    all_to_all x0 -> x1, starting transfers between devices: none -> 10.8 us  [shards(): lax.all_to_all(outbound, 'expert', split_axis=0, concat_axis=0, tiled=True)]
  transfers between devices with their start and end apart: 6 -> 9, of which waited for: 5 -> 6; matrix products, arithmetic and copies ran while one was open for 7% -> 11% of each run, Pallas kernels for 0% -> 0%
where the time goes in v1:
time: 446 us; the launch traced here: 445 us
  waiting for transfers between devices  316 us (71%)
  local copies, waits for them, and re-layouts  46.5 us (10%)
  matrix products  36.3 us (8%)
  starting transfers between devices  25.2 us (6%)
  between operations  13.4 us (3%)
  other arithmetic  8.07 us (2%)
    ppermute x2, waiting for transfers between devices, state_slot_on(): y2 = lax.ppermute(piece_out[-1], 'dp', all_rows)  107 us
    all_to_all x1, waiting for transfers between devices, shards(): lax.all_to_all(done, 'expert', split_axis=0, concat_axis=0, tiled=True)  95.8 us
    all_gather x1, waiting for transfers between devices, shards(): columns = lax.all_gather(w_out, 'expert', axis=1, tiled=True)  72.3 us
    reduce_scatter x1, waiting for transfers between devices, shards(): lax.psum_scatter(jnp.dot(context, columns, preferred_element_type=jnp.flo...  21.4 us
    dot_general x1, matrix products, shards(): jnp.dot(expert_mid, down_full[0], preferred_element_type=jnp.float32)  17.5 us
    all_gather x1, waiting for transfers between devices, fetch_experts(): lax.all_gather(w_down, 'dp', axis=1, tiled=True)  17.2 us
    unnamed x27, local copies, waits for them, and re-layouts  13 us
    all_to_all x1, starting transfers between devices, shards(): lax.all_to_all(done, 'expert', split_axis=0, concat_axis=0, tiled=True)  10.9 us
  transfers between devices with their start and end apart: 9, of which 6 were waited for; matrix products, arithmetic and copies ran while one was open for 11% of the time, Pallas kernels for 0%

profile of v1, /device:TPU:8, one launch (start us, length us, event | category | flops | bytes accessed | tf_op | source)
XLA Modules:
  0.0 445.0 jit_solution(4434382338128806184)
XLA Ops:
  6.5 0.7 all-gather.4.cloned.1.call-update
  7.3 0.0 reduce-scatter.2.cloned.1.call-start
  7.3 0.7 compare_select_fusion.1
  8.0 0.1 reshape.88
  8.1 1.7 slice_bitcast_fusion
  9.8 0.6 gather_fusion.1
  10.4 0.3 reshape.78
  10.7 0.8 reshape.79
  11.5 0.1 lt.43
  11.6 0.6 gather_fusion
  12.2 0.3 reshape.77
  12.5 0.1 iota_compare_fusion.1
  12.6 2.6 fusion.37
  15.2 1.6 fusion.19
  16.8 0.2 copy.43
  17.0 72.3 %all-gather.4.cloned.1.call-done = bf16[512,2048]{0,1:T(8,128)(2,1)} async-done(((bf16[512,32]{0,1:T(8,128)(2,1)}), bf16[512,2048]{0,1:T(8,128)(2,1)}) %all-gather.4.cloned.1.call-update) | async-done | bytes 2097168 | tf_op jit(solution)/shard_map/all_gather | solution.py:81
  89.3 3.3 convolution_convert_fusion.1
  92.7 0.0 all-gather.6.cloned.1.call-start
  92.7 0.7 all-gather.6.cloned.1.call-update
  93.4 0.0 all-gather.8.cloned.1.call-start
  93.5 0.5 all-gather.8.cloned.1.call-update
  94.0 0.1 copy.45
  94.1 0.1 eq.46
  94.3 0.1 eq.42
  94.4 0.9 reduce-window.6
  95.3 0.2 slice_reduce_fusion
  95.6 0.1 fusion.32
  95.7 0.1 reduce_sum.49
  95.8 0.1 copy.48
  95.9 0.3 fusion.18
  96.2 21.4 %reduce-scatter.2.cloned.1.call-done = bf16[64,2048]{1,0:T(8,128)(2,1)} async-done(((bf16[256,2048]{1,0:T(8,128)(2,1)}), bf16[64,2048]{1,0:T(8,128)(2,1)}) %reduce-scatter.2.cloned.1.call-update) | async-done | bytes 262160 | tf_op jit(solution)/shard_map/reduce_scatter | solution.py:82
  117.6 1.1 multiply_reduce_fusion.2
  118.8 2.0 convolution_convert_fusion
  120.8 2.7 reshape.82
  123.5 10.8 %all-to-all-start = ((bf16[64,12,2048]{2,1,0:T(8,128)(2,1)}), bf16[64,12,2048]{2,1,0:T(8,128)(2,1)}, u32[]{:S(2)}, u32[]{:S(2)}) async-start(bf16[64,12,2048]{2,1,0:T(8,128)(2,1)} %reshape.82), calls=%async_computation.1 | async-start | bytes 8388608 | tf_op jit(solution)/shard_map/all_to_all | solution.py:104
  134.3 0.1 collective-permute-start
  134.4 66.2 %collective-permute-done = bf16[1,512,1408]{2,1,0:T(8,128)(2,1)S(1)} collective-permute-done((bf16[1,512,1408]{2,1,0:T(8,128)(2,1)S(1)}, bf16[1,512,1408]{2,1,0:T(8,128)(2,1)S(1)}, u32[]{:S(2)}, u32[]{:S(2)}) %collective-permute-start) | collective-permute-done | bytes 1441824 | tf_op jit(solution)/shard_map/ppermute | solution.py:19
  200.7 3.2 collective-permute-start.2
  203.9 40.8 %collective-permute-done.1 = bf16[1,512,1408]{2,1,0:T(8,128)(2,1)} collective-permute-done((bf16[1,512,1408]{2,1,0:T(8,128)(2,1)S(1)}, bf16[1,512,1408]{2,1,0:T(8,128)(2,1)}, u32[]{:S(2)}, u32[]{:S(2)}) %collective-permute-start.1) | collective-permute-done | bytes 1441824 | tf_op jit(solution)/shard_map/ppermute | solution.py:19
  244.7 2.6 constant_dynamic-update-slice_fusion.7
  247.3 1.2 constant_dynamic-update-slice_fusion.6
  248.5 1.2 constant_dynamic-update-slice_fusion.5
  249.7 2.6 constant_dynamic-update-slice_fusion.4
  252.4 2.6 constant_dynamic-update-slice_fusion.3
  254.9 1.2 constant_dynamic-update-slice_fusion.2
  256.2 1.3 constant_dynamic-update-slice_fusion.1
  257.5 2.6 constant_dynamic-update-slice_fusion
  260.1 4.7 %reshape.83 = bf16[768,2048]{1,0:T(8,128)(2,1)S(1)} reshape(bf16[64,12,2048]{2,1,0:T(8,128)(2,1)} %all-to-all-done) | data formatting | bytes 6291456 | tf_op jit(solution)/shard_map/reshape | solution.py:105
  264.8 0.0 all-gather.6.cloned.1.call-done
  264.8 9.3 %fusion.3 = f32[768,1408]{1,0:T(8,128)} fusion(bf16[768,2048]{1,0:T(8,128)(2,1)S(1)} %reshape.83, bf16[1,2048,1408]{2,1,0:T(8,128)(2,1)} %all-gather.6.cloned.1.call-done), kind=kOutput, calls=%fused_computation.6 | convolution fusion | flops 4429185024 | bytes 13238272 | tf_op jit(solution)/shard_map/dot_general | solution.py:107
  274.2 17.2 %all-gather.8.cloned.1.call-done = bf16[1,1408,2048]{2,1,0:T(8,128)(2,1)} async-done(((bf16[1,352,2048]{2,1,0:T(8,128)(2,1)}), bf16[1,1408,2048]{2,1,0:T(8,128)(2,1)}) %all-gather.8.cloned.1.call-update) | async-done | bytes 5767184 | tf_op jit(solution)/shard_map/all_gather | solution.py:41
  291.3 17.5 %fusion.10 = bf16[768,2048]{1,0:T(8,128)(2,1)} fusion(bf16[1,1408,2048]{2,1,0:T(8,128)(2,1)} %all-gather.8.cloned.1.call-done, f32[768,1408]{1,0:T(8,128)} %fusion.3, bf16[768,2048]{1,0:T(8,128)(2,1)S(1)} %reshape.83, bf16[1,4096,1408]{2,1,0:T(8,128)(2,1)} %constant_dynamic-update-slice_fusion, s32[]{:T(128)S(6)} %select_n.31), kind=kOutput, calls=%fused_computation.14 | convolution fusion | flops 8866430976 | bytes 22151172 | tf_op jit(solution)/shard_map/dot_general | solution.py:109
  308.8 6.1 %reshape.84 = bf16[64,12,2048]{2,1,0:T(8,128)(2,1)} reshape(bf16[768,2048]{1,0:T(8,128)(2,1)} %fusion.10) | data formatting | bytes 6291456 | tf_op jit(solution)/shard_map/reshape | solution.py:112
  314.9 10.9 %all-to-all-start.1 = ((bf16[64,12,2048]{2,1,0:T(8,128)(2,1)}), bf16[64,12,2048]{2,1,0:T(8,128)(2,1)}, u32[]{:S(2)}, u32[]{:S(2)}) async-start(bf16[64,12,2048]{2,1,0:T(8,128)(2,1)} %reshape.84), calls=%async_computation.2 | async-start | bytes 8388608 | tf_op jit(solution)/shard_map/all_to_all | solution.py:113
  325.8 0.1 copy.49
  325.9 0.1 reshape.104
  326.0 0.1 copy.44
  326.1 95.8 %all-to-all-done.1 = bf16[64,12,2048]{2,1,0:T(8,128)(2,1)} async-done(((bf16[64,12,2048]{2,1,0:T(8,128)(2,1)}), bf16[64,12,2048]{2,1,0:T(8,128)(2,1)}, u32[]{:S(2)}, u32[]{:S(2)}) %all-to-all-start.1) | async-done | bytes 3145760 | tf_op jit(solution)/shard_map/all_to_all | solution.py:113
  421.9 4.7 %reshape.85 = bf16[768,2048]{1,0:T(8,128)(2,1)S(1)} reshape(bf16[64,12,2048]{2,1,0:T(8,128)(2,1)} %all-to-all-done.1) | data formatting | bytes 6291456 | tf_op jit(solution)/shard_map/reshape | solution.py:114
  426.6 3.1 gather_fusion.2
  429.7 3.9 reshape.118
  433.7 3.7 multiply_reduce_fusion
  437.4 0.2 multiply_reduce_fusion.1
  437.7 0.8 multiply_convert_fusion.1
  (30 shorter events, 0.2 us)
Async XLA Ops:
  6.5 4.2 copy-start.3
  6.5 82.8 %all-gather.4.cloned.1.call-start = ((), (), s32[]{:S(2)}) async-start(), calls=%async_computation.3 | async-start | bytes 2129920 | tf_op jit(solution)/shard_map/all_gather | solution.py:81
  7.3 110.3 %reduce-scatter.2.cloned.1.call-start = ((), (), s32[]{:S(2)}) async-start(), calls=%async_computation.4 | async-start | bytes 1310720 | tf_op jit(solution)/shard_map/reduce_scatter | solution.py:82
  8.1 3.4 copy-start.8
  16.8 77.2 %copy-start.4 = (s32[64,6]{0,1:T(8,128)S(1)}, s32[64,6]{0,1:T(8,128)}, u32[]{:S(2)}) copy-start(s32[64,6]{0,1:T(8,128)} %param.20) | copy-start | bytes 4612
  16.8 100.8 %copy-start.1 = (bf16[64,2048]{1,0:T(8,128)(2,1)S(1)}, bf16[64,2048]{1,0:T(8,128)(2,1)}, u32[]{:S(2)}) copy-start(bf16[64,2048]{1,0:T(8,128)(2,1)} %param.18) | copy-start | bytes 786436
  17.0 101.7 %copy-start.5 = (f32[2048]{0:T(1024)S(1)}, f32[2048]{0:T(1024)}, u32[]{:S(2)}) copy-start(f32[2048]{0:T(1024)} %param.19) | copy-start | bytes 24580
  92.7 172.2 %all-gather.6.cloned.1.call-start = ((), (), s32[]{:S(2)}) async-start(), calls=%async_computation.5 | async-start | bytes 7208960 | tf_op jit(solution)/shard_map/all_gather | solution.py:40
  93.4 197.9 %all-gather.8.cloned.1.call-start = ((), (), s32[]{:S(2)}) async-start(), calls=%async_computation.6 | async-start | bytes 7208960 | tf_op jit(solution)/shard_map/all_gather | solution.py:41
  123.5 10.8 %copy-start = (bf16[1,512,1408]{2,1,0:T(8,128)(2,1)S(1)}, bf16[1,512,1408]{2,1,0:T(8,128)(2,1)}, u32[]{:S(2)}) copy-start(bf16[1,512,1408]{2,1,0:T(8,128)(2,1)} %param.22) | copy-start | bytes 4325380
  123.5 136.6 %all-to-all-start = ((bf16[64,12,2048]{2,1,0:T(8,128)(2,1)}), bf16[64,12,2048]{2,1,0:T(8,128)(2,1)}, u32[]{:S(2)}, u32[]{:S(2)}) async-start(bf16[64,12,2048]{2,1,0:T(8,128)(2,1)} %reshape.82), calls=%async_computation.1 | async-start | bytes 8388608 | tf_op jit(solution)/shard_map/all_to_all | solution.py:104
  134.3 66.3 %collective-permute-start = (bf16[1,512,1408]{2,1,0:T(8,128)(2,1)S(1)}, bf16[1,512,1408]{2,1,0:T(8,128)(2,1)S(1)}, u32[]{:S(2)}, u32[]{:S(2)}) collective-permute-start(bf16[1,512,1408]{2,1,0:T(8,128)(2,1)S(1)} %copy-done), channel_id=1, source_target_pairs={{0,64},{64,128},{128,192},{192,0},{1,65},{65,129},{129,193},{193,1... | collective-permute-start | bytes 4325384 | tf_op jit(solution)/shard_map/ppermute | solution.py:19
  200.7 44.0 %collective-permute-start.1 = (bf16[1,512,1408]{2,1,0:T(8,128)(2,1)S(1)}, bf16[1,512,1408]{2,1,0:T(8,128)(2,1)}, u32[]{:S(2)}, u32[]{:S(2)}) collective-permute-start(bf16[1,512,1408]{2,1,0:T(8,128)(2,1)S(1)} %collective-permute-done), channel_id=1, source_target_pairs={{0,64},{64,128},{128,192},{192,0},{1,65},{65,129},{129,193},{193,1... | collective-permute-start | bytes 4325384 | tf_op jit(solution)/shard_map/ppermute | solution.py:19
  200.7 49.1 %collective-permute-start.2 = (bf16[1,512,1408]{2,1,0:T(8,128)(2,1)S(1)}, bf16[1,512,1408]{2,1,0:T(8,128)(2,1)}, u32[]{:S(2)}, u32[]{:S(2)}) collective-permute-start(bf16[1,512,1408]{2,1,0:T(8,128)(2,1)S(1)} %copy-done), channel_id=1, source_target_pairs={{0,192},{64,0},{128,64},{192,128},{1,193},{65,1},{129,65},{193,129... | collective-permute-start | bytes 4325384 | tf_op jit(solution)/shard_map/ppermute | solution.py:22
  314.9 11.1 %copy-start.7 = (f32[64,6]{0,1:T(8,128)S(1)}, f32[64,6]{0,1:T(8,128)}, u32[]{:S(2)}) copy-start(f32[64,6]{0,1:T(8,128)} %param.21) | copy-start | bytes 4612
  314.9 107.0 %all-to-all-start.1 = ((bf16[64,12,2048]{2,1,0:T(8,128)(2,1)}), bf16[64,12,2048]{2,1,0:T(8,128)(2,1)}, u32[]{:S(2)}, u32[]{:S(2)}) async-start(bf16[64,12,2048]{2,1,0:T(8,128)(2,1)} %reshape.84), calls=%async_computation.2 | async-start | bytes 8388608 | tf_op jit(solution)/shard_map/all_to_all | solution.py:113
  429.7 7.7 %copy-start.2 = (bf16[64,2048]{1,0:T(8,128)(2,1)S(1)}, bf16[64,2048]{1,0:T(8,128)(2,1)}, u32[]{:S(2)}) copy-start(bf16[64,2048]{1,0:T(8,128)(2,1)} %reduce-scatter.2.cloned.1.call-done) | copy-start | bytes 786436
  433.7 4.0 copy-start.6
Sparse Core Ops, SparseCore 0:
  10.1 79.1 all-gather.3
  92.8 24.7 reduce-scatter.1
  119.6 104.0 all-gather.5
  225.4 65.8 all-gather.7
